TPU v7x, 32 devices: a whole 2x2x4 slice. The times are simulated.
32 devices in a mesh: ctx: 4 (over y, x), vis: 8 (over z, core).
Axes of the slice: x: 2, y: 2, z: 4, core: 2. Of those that a mesh axis runs over, the one named last changes fastest.
Arguments:
- patches: bfloat16 [4096, 1280], P(('ctx', 'vis')), may hold values from -10 to 10
- vis_gain: float32 [1280], replicated, may hold values from 0.5 to 1.5
- w_qkv: bfloat16 [1280, 3840], P(None, 'vis'), may hold values from -2 to 2
- w_out: bfloat16 [1280, 1280], P('vis'), may hold values from -0.15625 to 0.15625
- merge_gain: float32 [1280], replicated, may hold values from 0.5 to 1.5
- w_merge: bfloat16 [5120, 8192], P(None, 'vis'), may hold values from -0.078125 to 0.078125
- token_dest: int32 [4, 256], replicated, may hold values from 0 to 3, as said below
- token_row: int32 [4, 256], replicated, may hold values from 0 to 1023, as said below
- prompt_text: bfloat16 [4096, 8192], P('ctx', 'vis'), may hold values from -6 to 6
- kv_gain: float32 [8192], P('vis'), may hold values from 0.5 to 1.5
- w_kv: bfloat16 [8192, 1024], P('vis'), may hold values from -1 to 1
- queries: bfloat16 [512, 4096], P('ctx'), may hold values from -12 to 12
- resp_kv: bfloat16 [512, 1024], P('ctx'), may hold values from -12 to 12
- resp_len: int32 [4], P('ctx'), may hold values from 64 to 128
Outputs:
- attended: bfloat16 [512, 4096], P('ctx')
Inputs may be any that keep to these rules, and one draw needn't show every extreme that they name: `token_dest`: the tokens of one image are in order of their prompt shard; at most 96 tokens of one image go to one shard, and from every image exactly 96 go to some shard. `token_row`: no two visual tokens take the same position of one shard.
All inputs are finite; a program needn't handle non-finite values.
Results may differ from a plain program's by a relative error of at most 0.014.
Values may be sent and summed in bfloat16 or wider, within the bound.
A program may use at most 128 MiB of HBM per device.

v0:
```python
import math
import jax
import jax.numpy as jnp
from jax import lax
from jax.sharding import PartitionSpec as P

VD = 1280
VHEADS = 16
D = 8192
HD = 128
QH = 32
KVH = 4
VHD = 80
MD = 5120
EPS = 1e-06


def merged_2(shard, axis, combine):
    everything = jax.tree.map(lambda part: lax.all_gather(part, axis), shard)
    initial = jax.tree.map(lambda part: part[0], everything)

    def lap(k, so_far):
        return combine(so_far, jax.tree.map(lambda part: part[k], everything))

    return lax.fori_loop(1, lax.axis_size(axis), lap, initial)


def layer_norm(values, gain):
    center = values - jnp.mean(values, axis=-1, keepdims=True)
    spread = jnp.mean(center * center, axis=-1, keepdims=True)
    return center * lax.rsqrt(spread + EPS) * gain


def dense_attention(query, keys, values):
    count = query.shape[0]
    block = min(512, count)
    scale = 1.0 / math.sqrt(query.shape[1])

    def one_block(part):
        scores = jnp.dot(part, keys.T, preferred_element_type=jnp.float32) * scale
        highest = jnp.max(scores, axis=1, keepdims=True)
        expo = jnp.exp(scores - highest)
        summed = jnp.sum(expo, axis=1, keepdims=True)
        mixed = jnp.dot(expo.astype(jnp.bfloat16), values, preferred_element_type=jnp.float32)
        return (mixed / summed).astype(jnp.bfloat16)

    blocks = query.reshape(count // block, block, query.shape[1])
    return lax.map(one_block, blocks).reshape(count, values.shape[1])


def head_attention(packed):
    stacked = jnp.transpose(packed, (1, 0, 2))

    def one_head(item):
        return dense_attention(item[:, :VHD], item[:, VHD : 2 * VHD], item[:, 2 * VHD :])

    return jnp.transpose(lax.map(one_head, stacked), (1, 0, 2))


def combine_partial(first, second):
    highest = jnp.maximum(first[0], second[0])
    fade_one = jnp.exp(first[0] - highest)
    fade_two = jnp.exp(second[0] - highest)
    return (
        highest,
        first[1] * fade_one + second[1] * fade_two,
        first[2] * fade_one[..., None] + second[2] * fade_two[..., None],
    )


def per_device(
    patches,
    vis_gain,
    w_qkv,
    w_out,
    merge_gain,
    w_merge,
    token_dest,
    token_row,
    prompt_text,
    kv_gain,
    w_kv,
    queries,
    resp_kv,
    resp_len,
):
    ctx_count = lax.axis_size("ctx")
    vis_count = lax.axis_size("vis")
    ctx_index = lax.axis_index("ctx")
    vis_index = lax.axis_index("vis")
    patch_count = patches.shape[0]
    floats = patches.astype(jnp.float32)
    normed = layer_norm(floats, vis_gain).astype(jnp.bfloat16)
    local_heads = VHEADS // vis_count
    qkv = jnp.dot(
        lax.all_gather(normed, "vis", axis=0, tiled=True), w_qkv, preferred_element_type=jnp.float32
    ).astype(jnp.bfloat16)
    image_rows = qkv.shape[0]
    heads = head_attention(qkv.reshape(image_rows, local_heads, 3 * VHD))
    returned = lax.all_to_all(heads, "vis", split_axis=0, concat_axis=1, tiled=True).reshape(
        patch_count, VD
    )
    projected = jnp.dot(
        returned,
        lax.all_gather(w_out, "vis", axis=0, tiled=True),
        preferred_element_type=jnp.float32,
    )
    mixed = floats + projected
    merged = layer_norm(mixed, merge_gain).astype(jnp.bfloat16).reshape(patch_count // 4, MD)
    visual = jnp.dot(
        lax.all_gather(merged, "vis", axis=0, tiled=True),
        w_merge,
        preferred_element_type=jnp.float32,
    ).astype(jnp.bfloat16)
    image_tokens = visual.shape[0]
    capacity = 3 * (image_tokens // ctx_count) // 2
    slots = jnp.arange(capacity, dtype=jnp.int32)
    shard_rows = prompt_text.shape[0]
    own_dest = lax.dynamic_index_in_dim(token_dest, ctx_index, 0, keepdims=False)
    shards = jnp.arange(ctx_count, dtype=jnp.int32)
    counts_out = jnp.sum((own_dest[None, :] == shards[:, None]).astype(jnp.int32), axis=1)
    starts_out = jnp.cumsum(counts_out) - counts_out
    picks = jnp.clip(starts_out[:, None] + slots[None, :], 0, image_tokens - 1).reshape(-1)
    filled = (slots[None, :] < counts_out[:, None]).reshape(-1, 1)
    outgoing = jnp.take(visual, picks, axis=0)
    outgoing = jnp.where(filled, outgoing, jnp.zeros_like(outgoing)).reshape(
        ctx_count, capacity, -1
    )
    arrived = lax.all_to_all(outgoing, "ctx", split_axis=0, concat_axis=0, tiled=True)
    pool = arrived.reshape(ctx_count * capacity, -1)
    firsts = jnp.sum((token_dest < ctx_index).astype(jnp.int32), axis=1)
    counts_in = jnp.sum((token_dest == ctx_index).astype(jnp.int32), axis=1)
    lookup = jnp.clip(firsts[:, None] + slots[None, :], 0, image_tokens - 1)
    places = jnp.take_along_axis(token_row, lookup, axis=1)
    live = slots[None, :] < counts_in[:, None]
    targets = jnp.where(live, places, shard_rows).reshape(-1)
    numbers = jnp.arange(ctx_count * capacity, dtype=jnp.int32) + 1
    source = jnp.zeros((shard_rows,), jnp.int32).at[targets].set(numbers, mode="drop")
    incoming = jnp.take(pool, jnp.maximum(source - 1, 0), axis=0)
    prompt = jnp.where((source > 0)[:, None], incoming, prompt_text)
    prompt_floats = prompt.astype(jnp.float32)
    squares = lax.psum(jnp.sum(prompt_floats * prompt_floats, axis=1), "vis")
    inverse = lax.rsqrt(squares / D + EPS)
    scaled = (prompt_floats * inverse[:, None] * kv_gain).astype(jnp.bfloat16)
    kv_share = lax.psum_scatter(
        jnp.dot(scaled, w_kv, preferred_element_type=jnp.float32),
        "vis",
        scatter_dimension=0,
        tiled=True,
    ).astype(jnp.bfloat16)
    width = KVH * HD
    group = QH // KVH
    resp_rows = queries.shape[0]
    scale = 1.0 / math.sqrt(HD)
    q_heads = queries.reshape(resp_rows, KVH, group, HD)

    def update(state, keys, values, visible):
        highest, summed, weighted = state
        scores = (
            jnp.einsum("rkgd,nkd->kgrn", q_heads, keys, preferred_element_type=jnp.float32) * scale
        )
        if visible is not None:
            scores = jnp.where(visible, scores, -1e30)
        new_high = jnp.maximum(highest, jnp.max(scores, axis=3))
        expo = jnp.exp(scores - new_high[..., None])
        if visible is not None:
            expo = jnp.where(visible, expo, 0.0)
        fade = jnp.exp(highest - new_high)
        summed = summed * fade + jnp.sum(expo, axis=3)
        weighted = weighted * fade[..., None] + jnp.einsum(
            "kgrn,nkd->kgrd", expo.astype(jnp.bfloat16), values, preferred_element_type=jnp.float32
        )
        return (new_high, summed, weighted)

    def fold_block(state, piece):
        count = piece.shape[0]
        return update(
            state,
            piece[:, :width].reshape(count, KVH, HD),
            piece[:, width:].reshape(count, KVH, HD),
            None,
        )

    def fold_prompt(state, piece):
        count = piece.shape[0]
        if count > 512 and count % 512 == 0:
            blocks = piece.reshape(count // 512, 512, 2 * width)

            def scan_step(inner, block):
                return (fold_block(inner, block), None)

            state, unused = lax.scan(scan_step, state, blocks)
            return state
        return fold_block(state, piece)

    own_count = resp_rows // vis_count
    own = lax.dynamic_slice_in_dim(resp_kv, vis_index * own_count, own_count, 0)
    key_positions = vis_index * own_count + jnp.arange(own_count, dtype=jnp.int32)
    query_positions = jnp.arange(resp_rows, dtype=jnp.int32)
    own_visible = key_positions[None, :] <= query_positions[:, None]
    start_state = (
        jnp.full((KVH, group, resp_rows), -1e30, jnp.float32),
        jnp.zeros((KVH, group, resp_rows), jnp.float32),
        jnp.zeros((KVH, group, resp_rows, HD), jnp.float32),
    )
    state = update(
        start_state,
        own[:, :width].reshape(own_count, KVH, HD),
        own[:, width:].reshape(own_count, KVH, HD),
        own_visible,
    )
    state = fold_prompt(state, lax.all_gather(kv_share, "ctx", axis=0, tiled=True))
    highest, summed, weighted = merged_2(state, "vis", combine_partial)
    result = weighted / summed[..., None]
    result = jnp.transpose(result, (2, 0, 1, 3)).reshape(resp_rows, QH * HD)
    live = (query_positions < resp_len[0])[:, None]
    return jnp.where(live, result, 0.0).astype(jnp.bfloat16)


def solution(mesh):
    return jax.shard_map(
        per_device,
        mesh=mesh,
        in_specs=(
            P(("ctx", "vis"), None),
            P(),
            P(None, "vis"),
            P("vis", None),
            P(),
            P(None, "vis"),
            P(),
            P(),
            P("ctx", "vis"),
            P("vis"),
            P("vis", None),
            P("ctx", None),
            P("ctx", None),
            P("ctx"),
        ),
        out_specs=P("ctx", None),
        check_vma=False,
    )
```

profile of v0, /device:TPU:0, one launch (start us, length us, event | category | flops | bytes accessed | tf_op | source)
XLA Modules:
  0.0 479.5 jit_solution(3582567656449933819)
XLA Ops:
  6.5 1.2 convert_reduce_fusion
  9.0 1.9 fusion.40
  11.8 35.8 %all-gather.7.cloned.1.call-done = bf16[1024,1280]{1,0:T(8,128)(2,1)} async-done(((bf16[128,1280]{1,0:T(8,128)(2,1)}), bf16[1024,1280]{1,0:T(8,128)(2,1)}) %all-gather.7.cloned.1.call-update) | async-done | bytes 2621456 | tf_op jit(solution)/shard_map/all_gather | solution.py:96
  47.5 3.5 convolution_convert_fusion
  51.1 1.3 copy.61
  52.4 11.1 %while.40 = (s32[]{:T(128)}, bf16[2,1024,80]{2,1,0:T(8,128)(2,1)}, bf16[2,1024,240]{2,1,0:T(8,128)(2,1)}, s32[]{:T(128)}, s32[]{:T(128)}, /*index=5*/s32[]{:T(128)}) while((s32[]{:T(128)}, bf16[2,1024,80]{2,1,0:T(8,128)(2,1)}, bf16[2,1024,240]{2,1,0:T(8,128)(2,1)}, s32[]{:T(128)}, s32[]{:T(128)}, /*index=5*/s32[]{:T(128)}) %tuple.93), condition=%wide.region_13.14_spmd, body=%wide.region_8.0_spmd.sunk | while | flops 172047360 | bytes 9758946 | solution.py:57
  53.7 3.3 while.42
  59.2 3.3 while.42
  63.5 1.6 copy.110
  65.1 31.0 %all_to_all.20 = bf16[1024,2,80]{2,1,0:T(2,128)(2,1)S(1)} all-to-all(bf16[1024,2,80]{2,1,0:T(2,128)(2,1)S(1)} %bitcast.150), channel_id=1, replica_groups=mesh['ctx'=4,'vis'=8] {'vis'}, dimensions={0} | all-to-all | bytes 655360 | tf_op jit(solution)/shard_map/all_to_all | solution.py:100
  96.5 2.4 all-gather.9.cloned.1.call-done
  98.9 2.7 fusion.72
  103.9 31.7 %all-gather.11.cloned.1.call-done = bf16[256,5120]{1,0:T(8,128)(2,1)} async-done(((bf16[32,5120]{1,0:T(8,128)(2,1)}), bf16[256,5120]{1,0:T(8,128)(2,1)}) %all-gather.11.cloned.1.call-update) | async-done | bytes 2621456 | tf_op jit(solution)/shard_map/all_gather | solution.py:111
  135.6 7.6 %convolution_convert_fusion.1 = bf16[256,1024]{1,0:T(8,128)(2,1)S(1)} fusion(bf16[256,5120]{1,0:T(8,128)(2,1)} %all-gather.11.cloned.1.call-done, bf16[5120,1024]{1,0:T(8,128)(2,1)} %param.25), kind=kOutput, calls=%fused_computation.52 | convolution fusion | flops 2684616704 | bytes 13631488 | tf_op jit(solution)/shard_map/dot_general | solution.py:110
  143.2 2.7 gather_fusion
  145.9 2.2 select_select_fusion.1
  148.1 3.6 all-to-all-start.1
  152.2 3.7 gather_fusion.2
  155.9 3.1 scatter_custom_fusion
  159.0 4.0 all-to-all-done.1
  163.1 5.4 %gather_fusion.1 = bf16[1024,1024]{1,0:T(8,128)(2,1)} fusion(bf16[384,1024]{1,0:T(8,128)(2,1)S(1)} %bitcast.141, s32[1024]{0:T(1024)S(1)} %fusion.55), kind=kCustom, calls=%fused_computation.1 | custom fusion | bytes 4198400 | tf_op jit(solution)/shard_map/jit(_take)/gather | solution.py:139
  168.4 4.1 fusion.19
  172.5 13.9 %psum.7 = f32[1024]{0:T(1024)S(1)} all-reduce(f32[1024]{0:T(1024)S(1)} %get-tuple-element.265), channel_id=1, replica_groups=mesh['ctx'=4,'vis'=8] {'vis'}, use_global_device_ids=true, to_apply=%region_17.18 | all-reduce | flops 1024 | bytes 8192 | tf_op jit(solution)/shard_map/psum | solution.py:142
  186.4 5.9 %fusion.26 = f32[1024,1024]{1,0:T(8,128)} fusion(bf16[1024,1024]{1,0:T(8,128)(2,1)S(1)} %copy-done, bf16[1024,1024]{1,0:T(8,128)(2,1)} %get-tuple-element.266, f32[1024]{0:T(1024)S(1)} %copy-done.5, f32[1024]{0:T(1024)S(1)} %add_rsqrt_fusion), kind=kOutput, calls=%fused_computation.43 | convolution fusion | flops 2151677952 | bytes 8396800 | tf_op jit(solution)/shard_map/dot_general | solution.py:146
  192.4 47.3 %reduce-scatter.2.cloned.1.call-done = f32[128,1024]{1,0:T(8,128)} async-done(((f32[1024,1024]{1,0:T(8,128)}), f32[128,1024]{1,0:T(8,128)}) %reduce-scatter.2.cloned.1.call-update) | async-done | bytes 524304 | tf_op jit(solution)/shard_map/reduce_scatter | solution.py:145
  239.7 1.8 convert_element_type.58
  241.6 1.4 copy.86
  244.3 22.3 %all-gather.13.cloned.1.call-done = bf16[512,1024]{1,0:T(8,128)(2,1)} async-done(((bf16[128,1024]{1,0:T(8,128)(2,1)}), bf16[512,1024]{1,0:T(8,128)(2,1)}) %all-gather.13.cloned.1.call-update) | async-done | bytes 1048592 | tf_op jit(solution)/shard_map/all_gather | solution.py:212
  266.6 2.3 fusion.70
  268.9 2.0 reshape.401
  270.8 5.5 %bitcast_reduce_fusion = (f32[4,8,128]{2,1,0:T(8,128)S(1)}, f32[4,512,128,8]{2,1,3,0:T(8,128)}) fusion(bf16[128,4,8,128]{3,2,1,0:T(8,128)(2,1)S(1)} %bitcast.145, bf16[512,4,128,1]{2,1,0,3:T(4,128)(2,1)} %bitcast.148), kind=kOutput, calls=%fused_computation.30 | convolution fusion | flops 541061120 | bytes 9977856 | tf_op jit(solution)/shard_map/rkgd,nkd->kgrn/dot_general | solution.py:160
  277.6 5.4 %fusion.22 = f32[4,8,128,128]{3,2,1,0:T(8,128)S(1)} fusion(f32[4,512,128,8]{2,1,3,0:T(8,128)} %get-tuple-element.289, f32[4,8,128]{2,1,0:T(8,128)S(1)} %get-tuple-element.277, bf16[512,4,128,1]{2,1,0,3:T(4,128)(2,1)S(1)} %bitcast.152), kind=kOutput, calls=%fused_computation.39 | convolution fusion | flops 543162368 | bytes 11026432 | tf_op jit(solution)/shard_map/kgrn,nkd->kgrd/dot_general | solution.py:170
  283.0 2.6 multiply_add_fusion
  286.3 4.8 %fusion.18 = f32[4,8,128]{2,1,0:T(8,128)S(1)} fusion(f32[4,512,128,8]{2,1,3,0:T(8,128)} %get-tuple-element.289, f32[4,8,128]{2,1,0:T(8,128)S(1)} %get-tuple-element.277), kind=kLoop, calls=%fused_computation.33 | loop fusion | flops 6287360 | bytes 8421376 | tf_op jit(solution)/shard_map/reduce_sum | solution.py:169
  291.2 14.7 %all_gather.30 = f32[8,4,8,128]{3,2,1,0:T(8,128)S(1)} all-gather(f32[1,4,8,128]{3,2,1,0:T(8,128)S(1)} %get-tuple-element.279), channel_id=1, replica_groups=mesh['ctx'=4,'vis'=8] {'vis'}, dimensions={0}, use_global_device_ids=true | all-gather | bytes 147456 | tf_op jit(solution)/shard_map/all_gather | solution.py:19
  305.8 21.1 %all_gather.31 = f32[8,4,8,128]{3,2,1,0:T(8,128)S(1)} all-gather(f32[1,4,8,128]{3,2,1,0:T(8,128)S(1)} %get-tuple-element.278), channel_id=1, replica_groups=mesh['ctx'=4,'vis'=8] {'vis'}, dimensions={0}, use_global_device_ids=true | all-gather | bytes 147456 | tf_op jit(solution)/shard_map/all_gather | solution.py:19
  326.9 111.4 %all-gather.15.cloned.1.call-done = f32[32,8,128,128]{3,2,1,0:T(8,128)} async-done(((f32[4,8,128,128]{3,2,1,0:T(8,128)}), f32[32,8,128,128]{3,2,1,0:T(8,128)}) %all-gather.15.cloned.1.call-update) | async-done | bytes 16777232 | tf_op jit(solution)/shard_map/all_gather | solution.py:19
  438.3 3.2 slice.51
  441.5 27.0 %while.41 = (s32[]{:T(128)}, f32[4,8,128]{2,1,0:T(8,128)S(1)}, f32[4,8,128]{2,1,0:T(8,128)S(1)}, f32[4,8,128,128]{3,2,1,0:T(8,128)}, f32[8,4,8,128]{3,2,1,0:T(8,...) while((s32[]{:T(128)}, f32[4,8,128]{2,1,0:T(8,128)S(1)}, ...), condition=%wide.region_23.24_spmd, body=%wide.region_22.23_spmd.sunk | while | flops 1597445 | bytes 6455447 | solution.py:25
  441.5 3.8 fusion.93
  445.4 3.8 fusion.93
  449.2 3.8 fusion.93
  453.1 3.8 fusion.93
  457.0 3.8 fusion.93
  460.8 3.8 fusion.93
  464.7 3.8 fusion.93
  468.5 1.9 divide_bitcast_fusion
  471.2 1.5 fusion.28
  (100 shorter events, 19.5 us)
Async XLA Ops:
  6.5 179.9 %copy-start = (bf16[1024,1024]{1,0:T(8,128)(2,1)S(1)}, bf16[1024,1024]{1,0:T(8,128)(2,1)}, u32[]{:S(2)}) copy-start(bf16[1024,1024]{1,0:T(8,128)(2,1)} %param.30) | copy-start | bytes 6291460
  6.5 41.0 %all-gather.7.cloned.1.call-start = ((), (), s32[]{:S(2)}) async-start(), calls=%async_computation.3 | async-start | bytes 2949120 | tf_op jit(solution)/shard_map/all_gather | solution.py:96
  11.0 87.9 %all-gather.9.cloned.1.call-start = ((), (), s32[]{:S(2)}) async-start(), calls=%async_computation.4 | async-start | bytes 3686400 | tf_op jit(solution)/shard_map/all_gather | solution.py:105
  11.7 123.8 %all-gather.11.cloned.1.call-start = ((), (), s32[]{:S(2)}) async-start(), calls=%async_computation.5 | async-start | bytes 2949120 | tf_op jit(solution)/shard_map/all_gather | solution.py:111
  63.5 35.4 %copy-start.2 = (bf16[128,1280]{1,0:T(8,128)(2,1)S(1)}, bf16[128,1280]{1,0:T(8,128)(2,1)}, u32[]{:S(2)}) copy-start(bf16[128,1280]{1,0:T(8,128)(2,1)} %param.20) | copy-start | bytes 983044
  98.9 2.9 copy-start.3
  101.6 1.4 copy-start.4
  145.9 6.3 %copy-start.1 = (s32[4,256]{1,0:T(4,128)S(1)}, s32[4,256]{1,0:T(4,128)}, u32[]{:S(2)}) copy-start(s32[4,256]{1,0:T(4,128)} %param.27) | copy-start | bytes 12292
  148.1 15.0 %all-to-all-start.1 = ((bf16[4,96,1024]{2,1,0:T(8,128)(2,1)}), bf16[4,96,1024]{2,1,0:T(8,128)(2,1)S(1)}, u32[]{:S(2)}, u32[]{:S(2)}) async-start(bf16[4,96,1024]{2,1,0:T(8,128)(2,1)} %select_select_fusion.1), calls=%async_computation.1 | async-start | bytes 1572864 | tf_op jit(solution)/shard_map/all_to_all | solution.py:129
  151.8 88.0 %reduce-scatter.2.cloned.1.call-start = ((), (), s32[]{:S(2)}) async-start(), calls=%async_computation.6 | async-start | bytes 4718592 | tf_op jit(solution)/shard_map/reduce_scatter | solution.py:145
  168.4 18.0 %copy-start.5 = (f32[1024]{0:T(1024)S(1)}, f32[1024]{0:T(1024)}, u32[]{:S(2)}) copy-start(f32[1024]{0:T(1024)} %param.29) | copy-start | bytes 12292
  192.4 74.3 %all-gather.13.cloned.1.call-start = ((), (), s32[]{:S(2)}) async-start(), calls=%async_computation.7 | async-start | bytes 1310720 | tf_op jit(solution)/shard_map/all_gather | solution.py:212
  241.5 196.8 %all-gather.15.cloned.1.call-start = ((), (), s32[]{:S(2)}) async-start(), calls=%async_computation.8 | async-start | bytes 18874368 | tf_op jit(solution)/shard_map/all_gather | solution.py:19
Sparse Core Ops, SparseCore 0:
  11.1 36.4 all-gather.6
  49.2 49.6 all-gather.8
  103.1 32.4 all-gather.10
  192.5 47.1 reduce-scatter.1
  241.6 24.9 all-gather.12
  285.7 152.5 all-gather.14
where the time goes:
time: 480 us; the launch traced here: 479 us
  waiting for transfers between devices  256 us (53%)
  blocking collectives  80.7 us (17%)
  other arithmetic  51.2 us (11%)
  matrix products  38.1 us (8%)
  local copies, waits for them, and re-layouts  35.4 us (7%)
  between operations  14.4 us (3%)
    all_gather x1, waiting for transfers between devices, merged_2(): everything = jax.tree.map(lambda part: lax.all_gather(part, axis), shard)  111 us
    reduce_scatter x1, waiting for transfers between devices, per_device(): lax.psum_scatter(jnp.dot(scaled, w_kv, preferred_element_type=jnp.float32...  47.3 us
    all_gather x2, blocking collectives, merged_2(): everything = jax.tree.map(lambda part: lax.all_gather(part, axis), shard)  35.8 us
    all_gather x1, waiting for transfers between devices, per_device(): lax.all_gather(normed, 'vis', axis=0, tiled=True)  35.8 us
    all_gather x1, waiting for transfers between devices, per_device(): lax.all_gather(merged, 'vis', axis=0, tiled=True)  31.7 us
    all_to_all x1, blocking collectives, per_device(): lax.all_to_all(heads, 'vis', split_axis=0, concat_axis=1, tiled=True)  31 us
    add x7, other arithmetic, combine_partial(): first[2] * fade_one[..., None] + second[2] * fade_two[..., None]  26.9 us
    all_gather x1, waiting for transfers between devices, per_device(): lax.all_gather(kv_share, 'ctx', axis=0, tiled=True)  22.3 us
  transfers between devices with their start and end apart: 7, of which 7 were waited for; matrix products, arithmetic and copies ran while one was open for 7% of the time, Pallas kernels for 0%

commit v1 on v0

--- a/solution.py
+++ b/solution.py
@@ -13,6 +13,36 @@
 VHD = 80
 MD = 5120
 EPS = 1e-06
+
+
+def fit_copies_up(view, k_dim):
+    view = jnp.moveaxis(view, 0, k_dim)
+    s_next = view.shape
+    e_now = view.reshape(*s_next[:k_dim], s_next[k_dim] * s_next[k_dim + 1], *s_next[k_dim + 2 :])
+    return e_now
+
+
+def convert_sides(panel, peer_axis):
+    b_next = jax.lax.axis_index(peer_axis)
+    d_next = jax.lax.axis_size(peer_axis)
+    frame_out, aux = (d_next, b_next)
+    u_next, q_next = (panel[None], 1)
+    while q_next < frame_out:
+        current_block = jax.lax.ppermute(
+            u_next, axis_name=peer_axis, perm=[(p, p ^ q_next) for p in range(frame_out)]
+        )
+        part_next = aux & q_next == 0
+        part_now = jnp.where(part_next, u_next, current_block)
+        main = jnp.where(part_next, current_block, u_next)
+        u_next = jnp.concatenate([part_now, main])
+        q_next *= 2
+    return u_next
+
+
+def handle_the_target(arr_in, mine, axis_k):
+    spare = convert_sides(arr_in, mine)
+    tile_out = fit_copies_up(spare, axis_k)
+    return tile_out
 
 
 def merged_2(shard, axis, combine):
@@ -108,9 +138,7 @@
     mixed = floats + projected
     merged = layer_norm(mixed, merge_gain).astype(jnp.bfloat16).reshape(patch_count // 4, MD)
     visual = jnp.dot(
-        lax.all_gather(merged, "vis", axis=0, tiled=True),
-        w_merge,
-        preferred_element_type=jnp.float32,
+        handle_the_target(merged, "vis", 0), w_merge, preferred_element_type=jnp.float32
     ).astype(jnp.bfloat16)
     image_tokens = visual.shape[0]
     capacity = 3 * (image_tokens // ctx_count) // 2

time: 480 us -> 529 us (1.10)
  waiting for transfers between devices: 256 us -> 301 us
    ppermute x0 -> x3, waiting for transfers between devices: none -> 76.8 us  [convert_sides(): jax.lax.ppermute(u_next, axis_name=peer_axis, perm=[(p, p ^ q_next) for p...]
    all_gather x1 -> x0, waiting for transfers between devices: 31.7 us -> none  [per_device(): lax.all_gather(merged, 'vis', axis=0, tiled=True)]
  transfers between devices with their start and end apart: 7 -> 9, of which waited for: 7 -> 9; matrix products, arithmetic and copies ran while one was open for 7% -> 6% of each run, Pallas kernels for 0% -> 0%
where the time goes in v1:
time: 529 us; the launch traced here: 528 us
  waiting for transfers between devices  301 us (57%)
  blocking collectives  80.2 us (15%)
  other arithmetic  55.6 us (11%)
  matrix products  37.3 us (7%)
  local copies, waits for them, and re-layouts  35.2 us (7%)
  between operations  14.1 us (3%)
    all_gather x1, waiting for transfers between devices, merged_2(): everything = jax.tree.map(lambda part: lax.all_gather(part, axis), shard)  112 us
    ppermute x3, waiting for transfers between devices, convert_sides(): jax.lax.ppermute(u_next, axis_name=peer_axis, perm=[(p, p ^ q_next) for p...  76.8 us
    reduce_scatter x1, waiting for transfers between devices, per_device(): lax.psum_scatter(jnp.dot(scaled, w_kv, preferred_element_type=jnp.float32...  47.3 us
    all_gather x1, waiting for transfers between devices, per_device(): lax.all_gather(normed, 'vis', axis=0, tiled=True)  35.8 us
    all_gather x2, blocking collectives, merged_2(): everything = jax.tree.map(lambda part: lax.all_gather(part, axis), shard)  35.6 us
    all_to_all x1, blocking collectives, per_device(): lax.all_to_all(heads, 'vis', split_axis=0, concat_axis=1, tiled=True)  31 us
    add x7, other arithmetic, combine_partial(): first[2] * fade_one[..., None] + second[2] * fade_two[..., None]  26.9 us
    all_gather x1, waiting for transfers between devices, per_device(): lax.all_gather(kv_share, 'ctx', axis=0, tiled=True)  22.3 us
  transfers between devices with their start and end apart: 9, of which 9 were waited for; matrix products, arithmetic and copies ran while one was open for 6% of the time, Pallas kernels for 0%

profile of v1, /device:TPU:0, one launch (start us, length us, event | category | flops | bytes accessed | tf_op | source)
XLA Modules:
  0.0 527.6 jit_solution(13517762090334433087)
XLA Ops:
  9.0 1.9 fusion.40
  11.7 35.8 %all-gather.6.cloned.1.call-done = bf16[1024,1280]{1,0:T(8,128)(2,1)} async-done(((bf16[128,1280]{1,0:T(8,128)(2,1)}), bf16[1024,1280]{1,0:T(8,128)(2,1)}) %all-gather.6.cloned.1.call-update) | async-done | bytes 2621456 | tf_op jit(solution)/shard_map/all_gather | solution.py:126
  47.5 3.5 convolution_convert_fusion
  52.4 11.1 %while.40 = (s32[]{:T(128)}, bf16[2,1024,80]{2,1,0:T(8,128)(2,1)}, bf16[2,1024,240]{2,1,0:T(8,128)(2,1)}, s32[]{:T(128)}, s32[]{:T(128)}, /*index=5*/s32[]{:T(128)}) while((s32[]{:T(128)}, bf16[2,1024,80]{2,1,0:T(8,128)(2,1)}, bf16[2,1024,240]{2,1,0:T(8,128)(2,1)}, s32[]{:T(128)}, s32[]{:T(128)}, /*index=5*/s32[]{:T(128)}) %tuple.96), condition=%wide.region_13.14_spmd, body=%wide.region_8.0_spmd.sunk | while | flops 172047360 | bytes 9758946 | solution.py:87
  53.7 3.3 while.42
  59.2 3.3 while.42
  63.5 1.6 copy.110
  65.1 31.0 %all_to_all.20 = bf16[1024,2,80]{2,1,0:T(2,128)(2,1)S(1)} all-to-all(bf16[1024,2,80]{2,1,0:T(2,128)(2,1)S(1)} %bitcast.152), channel_id=1, replica_groups=mesh['ctx'=4,'vis'=8] {'vis'}, dimensions={0} | all-to-all | bytes 655360 | tf_op jit(solution)/shard_map/all_to_all | solution.py:130
  96.5 2.4 all-gather.8.cloned.1.call-done
  98.9 2.7 fusion.72
  105.2 16.6 %collective-permute-done.1 = bf16[2,32,5120]{2,1,0:T(8,128)(2,1)} collective-permute-done((bf16[2,32,5120]{2,1,0:T(8,128)(2,1)S(1)}, bf16[2,32,5120]{2,1,0:T(8,128)(2,1)}, u32[]{:S(2)}, u32[]{:S(2)}) %collective-permute-start.1) | collective-permute-done | bytes 655392 | tf_op jit(solution)/shard_map/ppermute | solution.py:31
  124.9 58.8 %collective-permute-done.2 = bf16[4,32,5120]{2,1,0:T(8,128)(2,1)} collective-permute-done((bf16[4,32,5120]{2,1,0:T(8,128)(2,1)}, bf16[4,32,5120]{2,1,0:T(8,128)(2,1)}, u32[]{:S(2)}, u32[]{:S(2)}) %collective-permute-start.2) | collective-permute-done | bytes 1310752 | tf_op jit(solution)/shard_map/ppermute | solution.py:31
  183.7 1.5 broadcast_select_fusion.1
  185.4 6.8 %convolution_convert_fusion.1 = bf16[256,1024]{1,0:T(8,128)(2,1)S(1)} fusion(bf16[256,5120]{1,0:T(8,128)(2,1)S(1)} %bitcast.151, bf16[5120,1024]{1,0:T(8,128)(2,1)} %param.25), kind=kOutput, calls=%fused_computation.56 | convolution fusion | flops 2684616704 | bytes 13631488 | tf_op jit(solution)/shard_map/dot_general | solution.py:140
  192.2 2.7 gather_fusion
  194.9 2.2 select_select_fusion.1
  197.1 3.7 all-to-all-start.1
  201.3 3.7 gather_fusion.2
  205.0 2.9 scatter_custom_fusion
  208.0 3.9 all-to-all-done.1
  211.9 5.4 %gather_fusion.1 = bf16[1024,1024]{1,0:T(8,128)(2,1)} fusion(bf16[384,1024]{1,0:T(8,128)(2,1)S(1)} %bitcast.142, s32[1024]{0:T(1024)S(1)} %fusion.55), kind=kCustom, calls=%fused_computation.1 | custom fusion | bytes 4198400 | tf_op jit(solution)/shard_map/jit(_take)/gather | solution.py:167
  217.3 4.1 fusion.19
  221.3 13.6 %psum.7 = f32[1024]{0:T(1024)S(1)} all-reduce(f32[1024]{0:T(1024)S(1)} %get-tuple-element.265), channel_id=1, replica_groups=mesh['ctx'=4,'vis'=8] {'vis'}, use_global_device_ids=true, to_apply=%region_17.18 | all-reduce | flops 1024 | bytes 8192 | tf_op jit(solution)/shard_map/psum | solution.py:170
  234.9 5.9 %fusion.26 = f32[1024,1024]{1,0:T(8,128)} fusion(bf16[1024,1024]{1,0:T(8,128)(2,1)S(1)} %copy-done, bf16[1024,1024]{1,0:T(8,128)(2,1)} %get-tuple-element.266, f32[1024]{0:T(1024)S(1)} %copy-done.7, f32[1024]{0:T(1024)S(1)} %add_rsqrt_fusion), kind=kOutput, calls=%fused_computation.44 | convolution fusion | flops 2151677952 | bytes 8396800 | tf_op jit(solution)/shard_map/dot_general | solution.py:174
  240.9 47.3 %reduce-scatter.2.cloned.1.call-done = f32[128,1024]{1,0:T(8,128)} async-done(((f32[1024,1024]{1,0:T(8,128)}), f32[128,1024]{1,0:T(8,128)}) %reduce-scatter.2.cloned.1.call-update) | async-done | bytes 524304 | tf_op jit(solution)/shard_map/reduce_scatter | solution.py:173
  288.2 1.8 convert_element_type.58
  290.0 1.4 copy.86
  292.8 22.3 %all-gather.10.cloned.1.call-done = bf16[512,1024]{1,0:T(8,128)(2,1)} async-done(((bf16[128,1024]{1,0:T(8,128)(2,1)}), bf16[512,1024]{1,0:T(8,128)(2,1)}) %all-gather.10.cloned.1.call-update) | async-done | bytes 1048592 | tf_op jit(solution)/shard_map/all_gather | solution.py:240
  315.1 2.3 fusion.70
  317.3 2.0 reshape.401
  319.3 5.5 %bitcast_reduce_fusion = (f32[4,8,128]{2,1,0:T(8,128)S(1)}, f32[4,512,128,8]{2,1,3,0:T(8,128)}) fusion(bf16[128,4,8,128]{3,2,1,0:T(8,128)(2,1)S(1)} %bitcast.146, bf16[512,4,128,1]{2,1,0,3:T(4,128)(2,1)} %bitcast.149), kind=kOutput, calls=%fused_computation.30 | convolution fusion | flops 541061120 | bytes 9977856 | tf_op jit(solution)/shard_map/rkgd,nkd->kgrn/dot_general | solution.py:188
  326.0 5.4 %fusion.22 = f32[4,8,128,128]{3,2,1,0:T(8,128)S(1)} fusion(f32[4,512,128,8]{2,1,3,0:T(8,128)} %get-tuple-element.295, f32[4,8,128]{2,1,0:T(8,128)S(1)} %get-tuple-element.283, bf16[512,4,128,1]{2,1,0,3:T(4,128)(2,1)S(1)} %bitcast.154), kind=kOutput, calls=%fused_computation.39 | convolution fusion | flops 543162368 | bytes 11026432 | tf_op jit(solution)/shard_map/kgrn,nkd->kgrd/dot_general | solution.py:198
  331.4 2.6 multiply_add_fusion
  334.8 4.8 fusion.18
  339.6 14.9 %all_gather.26 = f32[8,4,8,128]{3,2,1,0:T(8,128)S(1)} all-gather(f32[1,4,8,128]{3,2,1,0:T(8,128)S(1)} %get-tuple-element.285), channel_id=1, replica_groups=mesh['ctx'=4,'vis'=8] {'vis'}, dimensions={0}, use_global_device_ids=true | all-gather | bytes 147456 | tf_op jit(solution)/shard_map/all_gather | solution.py:49
  354.5 20.7 %all_gather.27 = f32[8,4,8,128]{3,2,1,0:T(8,128)S(1)} all-gather(f32[1,4,8,128]{3,2,1,0:T(8,128)S(1)} %get-tuple-element.284), channel_id=1, replica_groups=mesh['ctx'=4,'vis'=8] {'vis'}, dimensions={0}, use_global_device_ids=true | all-gather | bytes 147456 | tf_op jit(solution)/shard_map/all_gather | solution.py:49
  375.2 111.6 %all-gather.12.cloned.1.call-done = f32[32,8,128,128]{3,2,1,0:T(8,128)} async-done(((f32[4,8,128,128]{3,2,1,0:T(8,128)}), f32[32,8,128,128]{3,2,1,0:T(8,128)}) %all-gather.12.cloned.1.call-update) | async-done | bytes 16777232 | tf_op jit(solution)/shard_map/all_gather | solution.py:49
  486.8 3.2 slice.51
  489.9 27.0 %while.41 = (s32[]{:T(128)}, f32[4,8,128]{2,1,0:T(8,128)S(1)}, f32[4,8,128]{2,1,0:T(8,128)S(1)}, f32[4,8,128,128]{3,2,1,0:T(8,128)}, f32[8,4,8,128]{3,2,1,0:T(8,...) while((s32[]{:T(128)}, f32[4,8,128]{2,1,0:T(8,128)S(1)}, ...), condition=%wide.region_23.24_spmd, body=%wide.region_22.23_spmd.sunk | while | flops 1597445 | bytes 6455447 | solution.py:55
  490.0 3.8 fusion.93
  493.8 3.8 fusion.93
  497.7 3.8 fusion.93
  501.5 3.8 fusion.93
  505.4 3.8 fusion.93
  509.3 3.8 fusion.93
  513.1 3.8 fusion.93
  517.0 1.9 divide_bitcast_fusion
  519.6 1.5 fusion.28
  (113 shorter events, 26.7 us)
Async XLA Ops:
  6.5 228.4 %copy-start = (bf16[1024,1024]{1,0:T(8,128)(2,1)S(1)}, bf16[1024,1024]{1,0:T(8,128)(2,1)}, u32[]{:S(2)}) copy-start(bf16[1024,1024]{1,0:T(8,128)(2,1)} %param.30) | copy-start | bytes 6291460
  6.5 41.0 %all-gather.6.cloned.1.call-start = ((), (), s32[]{:S(2)}) async-start(), calls=%async_computation.3 | async-start | bytes 2949120 | tf_op jit(solution)/shard_map/all_gather | solution.py:126
  11.0 87.9 %all-gather.8.cloned.1.call-start = ((), (), s32[]{:S(2)}) async-start(), calls=%async_computation.4 | async-start | bytes 3686400 | tf_op jit(solution)/shard_map/all_gather | solution.py:135
  63.5 35.4 %copy-start.2 = (bf16[128,1280]{1,0:T(8,128)(2,1)S(1)}, bf16[128,1280]{1,0:T(8,128)(2,1)}, u32[]{:S(2)}) copy-start(bf16[128,1280]{1,0:T(8,128)(2,1)} %param.20) | copy-start | bytes 983044
  98.9 2.9 copy-start.5
  101.8 3.0 copy-start.6
  102.2 1.7 collective-permute-start
  103.9 0.7 copy-start.3
  104.0 0.8 copy-start.4
  104.8 17.0 %collective-permute-start.1 = (bf16[2,32,5120]{2,1,0:T(8,128)(2,1)S(1)}, bf16[2,32,5120]{2,1,0:T(8,128)(2,1)}, u32[]{:S(2)}, u32[]{:S(2)}) collective-permute-start(bf16[2,32,5120]{2,1,0:T(8,128)(2,1)S(1)} %pad_maximum_fusion.2), channel_id=1, source_target_pairs={{0,2},{1,3},{2,0},{3,1},{4,6},{5,7},{6,4},{7,5},{8,10},{9,11},{10,... | collective-permute-start | bytes 1966088 | tf_op jit(solution)/shard_map/ppermute | solution.py:31
  124.3 59.3 %collective-permute-start.2 = (bf16[4,32,5120]{2,1,0:T(8,128)(2,1)}, bf16[4,32,5120]{2,1,0:T(8,128)(2,1)}, u32[]{:S(2)}, u32[]{:S(2)}) collective-permute-start(bf16[4,32,5120]{2,1,0:T(8,128)(2,1)} %pad_maximum_fusion.1), channel_id=1, source_target_pairs={{0,4},{1,5},{2,6},{3,7},{4,0},{5,1},{6,2},{7,3},{8,12},{9,13},{10,... | collective-permute-start | bytes 3932168 | tf_op jit(solution)/shard_map/ppermute | solution.py:31
  194.9 6.4 %copy-start.1 = (s32[4,256]{1,0:T(4,128)S(1)}, s32[4,256]{1,0:T(4,128)}, u32[]{:S(2)}) copy-start(s32[4,256]{1,0:T(4,128)} %param.27) | copy-start | bytes 12292
  197.1 14.7 %all-to-all-start.1 = ((bf16[4,96,1024]{2,1,0:T(8,128)(2,1)}), bf16[4,96,1024]{2,1,0:T(8,128)(2,1)S(1)}, u32[]{:S(2)}, u32[]{:S(2)}) async-start(bf16[4,96,1024]{2,1,0:T(8,128)(2,1)} %select_select_fusion.1), calls=%async_computation.1 | async-start | bytes 1572864 | tf_op jit(solution)/shard_map/all_to_all | solution.py:157
  200.8 87.4 %reduce-scatter.2.cloned.1.call-start = ((), (), s32[]{:S(2)}) async-start(), calls=%async_computation.5 | async-start | bytes 4718592 | tf_op jit(solution)/shard_map/reduce_scatter | solution.py:173
  217.3 17.7 %copy-start.7 = (f32[1024]{0:T(1024)S(1)}, f32[1024]{0:T(1024)}, u32[]{:S(2)}) copy-start(f32[1024]{0:T(1024)} %param.29) | copy-start | bytes 12292
  240.8 74.2 %all-gather.10.cloned.1.call-start = ((), (), s32[]{:S(2)}) async-start(), calls=%async_computation.6 | async-start | bytes 1310720 | tf_op jit(solution)/shard_map/all_gather | solution.py:240
  290.0 196.8 %all-gather.12.cloned.1.call-start = ((), (), s32[]{:S(2)}) async-start(), calls=%async_computation.7 | async-start | bytes 18874368 | tf_op jit(solution)/shard_map/all_gather | solution.py:49
Sparse Core Ops, SparseCore 0:
  11.1 36.4 all-gather.5
  49.2 49.6 all-gather.7
  241.0 47.1 reduce-scatter.1
  290.1 24.9 all-gather.9
  334.1 152.5 all-gather.11
